TPU v7x, 128 devices: a whole 4x4x4 slice. The times are simulated.
128 devices in a mesh: dom: 32 (over x_lo, z, y), rep: 4 (over x_hi, core).
Axes of the slice: x: 4 (x_hi: 2, x_lo: 2; x = x_hi * 2 + x_lo), y: 4, z: 4, core: 2. Of those that a mesh axis runs over, the one named last changes fastest.
Arguments:
- features: bfloat16 [49152, 256], P('dom'), may hold values from -6 to 6
- tile_weights: bfloat16 [32, 4, 8, 88, 128, 128], P('dom', 'rep'), may hold values from 0 to 0.0115356445
- tile_rows: int32 [32, 4, 8, 88], P('dom', 'rep'), may hold values from 0 to 11, as said below
- tile_cols: int32 [32, 4, 8, 88], P('dom', 'rep'), may hold values from 0 to 11, as said below
- tile_counts: int32 [32, 4, 8], P('dom', 'rep'), may hold values from 1 to 88, as said below
- weight_self: bfloat16 [256, 256], replicated, may hold values from -0.375 to 0.375
- weight_neigh: bfloat16 [256, 256], replicated, may hold values from -0.375 to 0.375
- cotangent: bfloat16 [49152, 256], P(('dom', 'rep')), may hold values from -0.026977539 to 0.026977539
Outputs:
- out: bfloat16 [49152, 256], P(('dom', 'rep'))
- grad_self: float32 [256, 256], replicated
- grad_neigh: float32 [256, 256], replicated
Inputs may be any that keep to these rules, and one draw needn't show every extreme that they name: For each p, r, s the first tile_counts[p, r, s] slots name distinct pairs (tile_rows, tile_cols); slots from tile_counts[p, r, s] on are unused. `tile_cols`: see tile_rows. `tile_counts`: some device fills all 88 slots of some column step.
All inputs are finite; a program needn't handle non-finite values.
Results may differ from a plain program's by a relative error of at most 0.0052.
Values may be sent and summed in bfloat16 or wider, within the bound.
A program may use at most 128 MiB of HBM per device.

v0:
```python
import jax
import jax.numpy as jnp
from jax import lax
from jax.sharding import PartitionSpec as P


def passed_along(block, axis, distance):
    devices = range(lax.axis_size(axis))
    route = [((i - distance) % len(devices), i) for i in devices]
    return lax.ppermute(block, axis, route)


def step_terms(feature_block, weights_dev, rows_dev, cols_dev, counts_dev, column_step):
    weights_now = lax.dynamic_index_in_dim(weights_dev, column_step, 0, keepdims=False)
    row_index = lax.dynamic_index_in_dim(rows_dev, column_step, 0, keepdims=False)
    col_index = lax.dynamic_index_in_dim(cols_dev, column_step, 0, keepdims=False)
    live_total = lax.dynamic_index_in_dim(counts_dev, column_step, 0, keepdims=False)
    slot_total = weights_now.shape[0]
    tile_side = weights_now.shape[1]
    width = feature_block.shape[1]
    row_tiles = feature_block.shape[0] // tile_side
    flat_block = feature_block.reshape(row_tiles, tile_side * width)
    tile_ids = jnp.arange(row_tiles, dtype=jnp.int32)
    select = (col_index[:, None] == tile_ids[None, :]).astype(jnp.bfloat16)
    picked = jnp.dot(select, flat_block, preferred_element_type=jnp.float32).astype(jnp.bfloat16)
    picked = picked.reshape(slot_total, tile_side, width)
    product = jnp.einsum("kij,kjf->kif", weights_now, picked, preferred_element_type=jnp.float32)
    live_slots = jnp.arange(slot_total, dtype=jnp.int32) < live_total
    placing = ((row_index[None, :] == tile_ids[:, None]) & live_slots[None, :]).astype(jnp.float32)
    summed = jnp.dot(
        placing,
        product.reshape(slot_total, tile_side * width),
        precision=lax.Precision.HIGHEST,
        preferred_element_type=jnp.float32,
    )
    return summed.reshape(feature_block.shape[0], width)


def rotate(feature_block, steps_per_group, offset, direction_sign):
    replica = lax.axis_index("rep")
    bit_total = (lax.axis_size("rep") - 1).bit_length()
    domain = lax.axis_size("dom")
    moves = []
    moves.append((offset % domain, -1))
    for bit_number in range(bit_total):
        moves.append((direction_sign * steps_per_group * (1 << bit_number) % domain, bit_number))
    for amount, bit_number in moves:
        shifted = passed_along(feature_block, "dom", amount)
        if bit_number < 0:
            feature_block = shifted
        else:
            flag = replica >> bit_number & 1 == 1
            feature_block = jnp.where(flag, shifted, feature_block)
    return feature_block


def move_up(feature_block):
    return passed_along(feature_block, "dom", -1)


def on_device(
    features, tile_weights, tile_rows, tile_cols, tile_counts, weight_self, weight_neigh, cotangent
):
    weights_dev = tile_weights[0, 0]
    rows_dev = tile_rows[0, 0]
    cols_dev = tile_cols[0, 0]
    counts_dev = tile_counts[0, 0]
    steps_per_group = weights_dev.shape[0]
    middle = steps_per_group // 2

    def contribution(feature_block, column_step):
        return step_terms(feature_block, weights_dev, rows_dev, cols_dev, counts_dev, column_step)

    empty = jnp.zeros(features.shape, jnp.float32)
    begin = rotate(features, steps_per_group, middle, -1)

    def turn_one(turn_index, carry):
        current, partial_value = carry
        partial_value = partial_value + contribution(current, turn_index)
        return (move_up(current), partial_value)

    current, partial_value = lax.fori_loop(0, steps_per_group - 1, turn_one, (begin, empty))
    partial_value = partial_value + contribution(current, steps_per_group - 1)
    aggregate = lax.psum_scatter(partial_value, "rep", scatter_dimension=0, tiled=True).astype(
        jnp.bfloat16
    )
    quarter = features.shape[0] // lax.axis_size("rep")
    own_rows = lax.dynamic_slice_in_dim(features, lax.axis_index("rep") * quarter, quarter, 0)
    pre = jnp.dot(own_rows, weight_self, preferred_element_type=jnp.float32)
    pre = pre + jnp.dot(aggregate, weight_neigh, preferred_element_type=jnp.float32)
    output = jax.nn.silu(pre).astype(jnp.bfloat16)
    sigmoid = jax.nn.sigmoid(pre)
    slope = (cotangent.astype(jnp.float32) * sigmoid * (1.0 + pre * (1.0 - sigmoid))).astype(
        jnp.bfloat16
    )
    self_term = jnp.einsum("nf,ng->fg", own_rows, slope, preferred_element_type=jnp.float32)
    neigh_term = jnp.einsum("nf,ng->fg", aggregate, slope, preferred_element_type=jnp.float32)
    grad_self, grad_neigh = lax.psum((self_term, neigh_term), ("dom", "rep"))
    return (output, grad_self, grad_neigh)


def solution(mesh):
    return jax.shard_map(
        on_device,
        mesh=mesh,
        in_specs=(
            P("dom", None),
            P("dom", "rep", None, None, None, None),
            P("dom", "rep", None, None),
            P("dom", "rep", None, None),
            P("dom", "rep", None),
            P(),
            P(),
            P(("dom", "rep"), None),
        ),
        out_specs=(P(("dom", "rep"), None), P(), P()),
        check_vma=False,
    )
```

profile of v0, /device:TPU:1, one launch (start us, length us, event | category | flops | bytes accessed | tf_op | source)
XLA Modules:
  0.0 608.2 jit_solution(17502834930815847477)
XLA Ops:
  7.2 2.5 collective-permute-start.1
  9.7 20.5 %collective-permute-done.1 = bf16[1536,256]{1,0:T(8,128)(2,1)S(1)} collective-permute-done((bf16[1536,256]{1,0:T(8,128)(2,1)}, bf16[1536,256]{1,0:T(8,128)(2,1)S(1)}, u32[]{:S(2)}, u32[]{:S(2)}) %collective-permute-start.1) | collective-permute-done | bytes 786464 | tf_op jit(solution)/shard_map/ppermute | solution.py:10
  31.3 18.3 %collective-permute-done.2 = bf16[1536,256]{1,0:T(8,128)(2,1)S(1)} collective-permute-done((bf16[1536,256]{1,0:T(8,128)(2,1)S(1)}, bf16[1536,256]{1,0:T(8,128)(2,1)S(1)}, u32[]{:S(2)}, u32[]{:S(2)}) %collective-permute-start.2) | collective-permute-done | bytes 786464 | tf_op jit(solution)/shard_map/ppermute | solution.py:10
  53.1 13.7 %collective-permute-done.3 = bf16[1536,256]{1,0:T(8,128)(2,1)S(1)} collective-permute-done((bf16[1536,256]{1,0:T(8,128)(2,1)S(1)}, bf16[1536,256]{1,0:T(8,128)(2,1)S(1)}, u32[]{:S(2)}, u32[]{:S(2)}) %collective-permute-start.3) | collective-permute-done | bytes 786464 | tf_op jit(solution)/shard_map/ppermute | solution.py:10
  67.8 301.9 %while.16 = (s32[]{:T(128)}, bf16[1536,256]{1,0:T(8,128)(2,1)}, f32[1536,256]{1,0:T(8,128)}, s32[8,88]{1,0:T(8,128)}, s32[8]{0:T(128)}, /*index=5*/bf16[8,88,128...) while((s32[]{:T(128)}, bf16[1536,256]{1,0:T(8,128)(2,1)}, f32[1536,256]{1,0:T(8,128)}, ...), condition=%wide.region_1.2_spmd.clone, body=%wide.region_0.1_spmd.clone.sunk | while | flops 1226312832 | bytes 88607792 | solution.py:82
  69.0 3.9 collective-permute-start
  74.2 1.7 convolution_convert_fusion.3
  75.8 1.5 copy.22
  77.4 7.8 %fusion.53 = f32[88,128,256]{2,1,0:T(8,128)} fusion(bf16[88,128,256]{2,1,0:T(8,128)(2,1)S(1)} %bitcast.64, bf16[8,88,128,128]{3,2,1,0:T(8,128)(2,1)} %get-tuple-element.244, s32[]{:T(128)} %get-tuple-element.230), kind=kOutput, calls=%fused_computation.1.clone.1 | convolution fusion | flops 738197504 | bytes 20185600 | tf_op jit(solution)/shard_map/while/body/eval_jaxpr/kij,kjf->kif/dot_general | solution.py:27
  85.2 16.1 %copy.23 = f32[11,8,128,256]{3,1,2,0:T(8,128)} copy(f32[11,8,128,256]{3,2,1,0:T(8,128)} %bitcast.62) | data formatting | bytes 23068672 | tf_op jit(solution)/shard_map/while
  102.5 6.7 %fusion.54 = f32[12,32768]{1,0:T(8,128)S(1)} fusion(f32[88,32768]{1,0:T(8,128)} %bitcast.61, s32[88]{0:T(128)S(1)} %get-tuple-element.220, pred[88]{0:T(512)(128)(4,1)S(1)} %iota_compare_fusion.11), kind=kOutput, calls=%fused_computation.9.clone.1 | convolution fusion | flops 415238208 | bytes 13107640 | tf_op jit(solution)/shard_map/while/body/eval_jaxpr/dot_general | solution.py:30
  110.6 2.8 select_add_fusion.2
  116.2 1.7 convolution_convert_fusion.3
  117.9 1.5 copy.22
  119.4 7.8 %fusion.53 = f32[88,128,256]{2,1,0:T(8,128)} fusion(bf16[88,128,256]{2,1,0:T(8,128)(2,1)S(1)} %bitcast.64, bf16[8,88,128,128]{3,2,1,0:T(8,128)(2,1)} %get-tuple-element.244, s32[]{:T(128)} %get-tuple-element.230), kind=kOutput, calls=%fused_computation.1.clone.1 | convolution fusion | flops 738197504 | bytes 20185600 | tf_op jit(solution)/shard_map/while/body/eval_jaxpr/kij,kjf->kif/dot_general | solution.py:27
  127.2 16.1 %copy.23 = f32[11,8,128,256]{3,1,2,0:T(8,128)} copy(f32[11,8,128,256]{3,2,1,0:T(8,128)} %bitcast.62) | data formatting | bytes 23068672 | tf_op jit(solution)/shard_map/while
  144.6 6.7 %fusion.54 = f32[12,32768]{1,0:T(8,128)S(1)} fusion(f32[88,32768]{1,0:T(8,128)} %bitcast.61, s32[88]{0:T(128)S(1)} %get-tuple-element.220, pred[88]{0:T(512)(128)(4,1)S(1)} %iota_compare_fusion.11), kind=kOutput, calls=%fused_computation.9.clone.1 | convolution fusion | flops 415238208 | bytes 13107640 | tf_op jit(solution)/shard_map/while/body/eval_jaxpr/dot_general | solution.py:30
  152.6 3.2 select_add_fusion.2
  158.4 1.7 convolution_convert_fusion.3
  160.1 1.5 copy.22
  161.7 7.8 %fusion.53 = f32[88,128,256]{2,1,0:T(8,128)} fusion(bf16[88,128,256]{2,1,0:T(8,128)(2,1)S(1)} %bitcast.64, bf16[8,88,128,128]{3,2,1,0:T(8,128)(2,1)} %get-tuple-element.244, s32[]{:T(128)} %get-tuple-element.230), kind=kOutput, calls=%fused_computation.1.clone.1 | convolution fusion | flops 738197504 | bytes 20185600 | tf_op jit(solution)/shard_map/while/body/eval_jaxpr/kij,kjf->kif/dot_general | solution.py:27
  169.4 16.1 %copy.23 = f32[11,8,128,256]{3,1,2,0:T(8,128)} copy(f32[11,8,128,256]{3,2,1,0:T(8,128)} %bitcast.62) | data formatting | bytes 23068672 | tf_op jit(solution)/shard_map/while
  186.8 6.7 %fusion.54 = f32[12,32768]{1,0:T(8,128)S(1)} fusion(f32[88,32768]{1,0:T(8,128)} %bitcast.61, s32[88]{0:T(128)S(1)} %get-tuple-element.220, pred[88]{0:T(512)(128)(4,1)S(1)} %iota_compare_fusion.11), kind=kOutput, calls=%fused_computation.9.clone.1 | convolution fusion | flops 415238208 | bytes 13107640 | tf_op jit(solution)/shard_map/while/body/eval_jaxpr/dot_general | solution.py:30
  194.9 3.2 select_add_fusion.2
  200.6 1.7 convolution_convert_fusion.3
  202.3 1.5 copy.22
  203.9 7.8 %fusion.53 = f32[88,128,256]{2,1,0:T(8,128)} fusion(bf16[88,128,256]{2,1,0:T(8,128)(2,1)S(1)} %bitcast.64, bf16[8,88,128,128]{3,2,1,0:T(8,128)(2,1)} %get-tuple-element.244, s32[]{:T(128)} %get-tuple-element.230), kind=kOutput, calls=%fused_computation.1.clone.1 | convolution fusion | flops 738197504 | bytes 20185600 | tf_op jit(solution)/shard_map/while/body/eval_jaxpr/kij,kjf->kif/dot_general | solution.py:27
  211.7 16.1 %copy.23 = f32[11,8,128,256]{3,1,2,0:T(8,128)} copy(f32[11,8,128,256]{3,2,1,0:T(8,128)} %bitcast.62) | data formatting | bytes 23068672 | tf_op jit(solution)/shard_map/while
  229.0 6.7 %fusion.54 = f32[12,32768]{1,0:T(8,128)S(1)} fusion(f32[88,32768]{1,0:T(8,128)} %bitcast.61, s32[88]{0:T(128)S(1)} %get-tuple-element.220, pred[88]{0:T(512)(128)(4,1)S(1)} %iota_compare_fusion.11), kind=kOutput, calls=%fused_computation.9.clone.1 | convolution fusion | flops 415238208 | bytes 13107640 | tf_op jit(solution)/shard_map/while/body/eval_jaxpr/dot_general | solution.py:30
  237.1 3.2 select_add_fusion.2
  241.5 2.6 collective-permute-start
  245.3 1.7 convolution_convert_fusion.3
  247.0 1.5 copy.22
  248.5 7.8 %fusion.53 = f32[88,128,256]{2,1,0:T(8,128)} fusion(bf16[88,128,256]{2,1,0:T(8,128)(2,1)S(1)} %bitcast.64, bf16[8,88,128,128]{3,2,1,0:T(8,128)(2,1)} %get-tuple-element.244, s32[]{:T(128)} %get-tuple-element.230), kind=kOutput, calls=%fused_computation.1.clone.1 | convolution fusion | flops 738197504 | bytes 20185600 | tf_op jit(solution)/shard_map/while/body/eval_jaxpr/kij,kjf->kif/dot_general | solution.py:27
  256.3 16.1 %copy.23 = f32[11,8,128,256]{3,1,2,0:T(8,128)} copy(f32[11,8,128,256]{3,2,1,0:T(8,128)} %bitcast.62) | data formatting | bytes 23068672 | tf_op jit(solution)/shard_map/while
  273.7 6.7 %fusion.54 = f32[12,32768]{1,0:T(8,128)S(1)} fusion(f32[88,32768]{1,0:T(8,128)} %bitcast.61, s32[88]{0:T(128)S(1)} %get-tuple-element.220, pred[88]{0:T(512)(128)(4,1)S(1)} %iota_compare_fusion.11), kind=kOutput, calls=%fused_computation.9.clone.1 | convolution fusion | flops 415238208 | bytes 13107640 | tf_op jit(solution)/shard_map/while/body/eval_jaxpr/dot_general | solution.py:30
  281.7 3.2 select_add_fusion.2
  287.8 1.7 convolution_convert_fusion.3
  289.5 1.5 copy.22
  291.0 7.8 %fusion.53 = f32[88,128,256]{2,1,0:T(8,128)} fusion(bf16[88,128,256]{2,1,0:T(8,128)(2,1)S(1)} %bitcast.64, bf16[8,88,128,128]{3,2,1,0:T(8,128)(2,1)} %get-tuple-element.244, s32[]{:T(128)} %get-tuple-element.230), kind=kOutput, calls=%fused_computation.1.clone.1 | convolution fusion | flops 738197504 | bytes 20185600 | tf_op jit(solution)/shard_map/while/body/eval_jaxpr/kij,kjf->kif/dot_general | solution.py:27
  298.8 16.1 %copy.23 = f32[11,8,128,256]{3,1,2,0:T(8,128)} copy(f32[11,8,128,256]{3,2,1,0:T(8,128)} %bitcast.62) | data formatting | bytes 23068672 | tf_op jit(solution)/shard_map/while
  316.2 6.7 %fusion.54 = f32[12,32768]{1,0:T(8,128)S(1)} fusion(f32[88,32768]{1,0:T(8,128)} %bitcast.61, s32[88]{0:T(128)S(1)} %get-tuple-element.220, pred[88]{0:T(512)(128)(4,1)S(1)} %iota_compare_fusion.11), kind=kOutput, calls=%fused_computation.9.clone.1 | convolution fusion | flops 415238208 | bytes 13107640 | tf_op jit(solution)/shard_map/while/body/eval_jaxpr/dot_general | solution.py:30
  324.2 3.2 select_add_fusion.2
  330.0 1.7 convolution_convert_fusion.3
  331.7 1.5 copy.22
  333.3 7.8 %fusion.53 = f32[88,128,256]{2,1,0:T(8,128)} fusion(bf16[88,128,256]{2,1,0:T(8,128)(2,1)S(1)} %bitcast.64, bf16[8,88,128,128]{3,2,1,0:T(8,128)(2,1)} %get-tuple-element.244, s32[]{:T(128)} %get-tuple-element.230), kind=kOutput, calls=%fused_computation.1.clone.1 | convolution fusion | flops 738197504 | bytes 20185600 | tf_op jit(solution)/shard_map/while/body/eval_jaxpr/kij,kjf->kif/dot_general | solution.py:27
  341.1 16.1 %copy.23 = f32[11,8,128,256]{3,1,2,0:T(8,128)} copy(f32[11,8,128,256]{3,2,1,0:T(8,128)} %bitcast.62) | data formatting | bytes 23068672 | tf_op jit(solution)/shard_map/while
  358.4 6.7 %fusion.54 = f32[12,32768]{1,0:T(8,128)S(1)} fusion(f32[88,32768]{1,0:T(8,128)} %bitcast.61, s32[88]{0:T(128)S(1)} %get-tuple-element.220, pred[88]{0:T(512)(128)(4,1)S(1)} %iota_compare_fusion.11), kind=kOutput, calls=%fused_computation.9.clone.1 | convolution fusion | flops 415238208 | bytes 13107640 | tf_op jit(solution)/shard_map/while/body/eval_jaxpr/dot_general | solution.py:30
  366.5 3.2 select_add_fusion.2
  369.7 1.6 reshape.66
  371.3 1.7 convolution_convert_fusion.1
  373.0 1.5 copy.17
  374.5 8.6 %convolution_bitcast_fusion = f32[88,128,256]{1,2,0:T(8,128)} fusion(bf16[88,128,256]{2,1,0:T(8,128)(2,1)S(1)} %bitcast.68, bf16[1,1,8,88,128,128]{5,4,3,2,1,0:T(8,128)(2,1)} %bitcast.70), kind=kOutput, calls=%fused_computation.19 | convolution fusion | flops 738197504 | bytes 20185088 | tf_op jit(solution)/shard_map/kij,kjf->kif/dot_general | solution.py:27
  383.1 12.2 %copy.18 = f32[11,8,128,256]{3,1,2,0:T(8,128)} copy(f32[11,8,128,256]{2,3,1,0:T(8,128)} %bitcast.66) | data formatting | bytes 23068672
  395.3 8.2 %fusion.23 = f32[12,32768]{1,0:T(8,128)} fusion(f32[88,32768]{1,0:T(8,128)} %bitcast.65, s32[88]{0:T(128)S(1)} %slice_bitcast_fusion.1, pred[88]{0:T(512)(128)(4,1)S(1)} %iota_compare_fusion.7), kind=kOutput, calls=%fused_computation.39 | convolution fusion | flops 415238208 | bytes 13107640 | tf_op jit(solution)/shard_map/dot_general | solution.py:30
  403.5 1.9 reshape.69
  405.4 1.4 add.62
  407.9 37.6 %reduce-scatter.2.cloned.1.call-done = f32[384,256]{1,0:T(8,128)} async-done(((f32[1536,256]{1,0:T(8,128)}), f32[384,256]{1,0:T(8,128)}) %reduce-scatter.2.cloned.1.call-update) | async-done | bytes 393232 | tf_op jit(solution)/shard_map/reduce_scatter | solution.py:84
  445.6 2.1 multiply_convert_fusion
  447.6 1.9 fusion.14
  449.5 2.0 fusion.18
  451.5 146.5 %all-reduce.3.cloned.1.call-done = (f32[256,256]{1,0:T(8,128)}, f32[256,256]{1,0:T(8,128)}) async-done(((f32[256,256]{1,0:T(8,128)}, f32[256,256]{1,0:T(8,128)}), (f32[256,256]{1,0:T(8,128)}, f32[256,256]{1,0:T(8,128)})) %all-reduce.3.cloned.1.call-update) | async-done | bytes 524304 | tf_op jit(solution)/shard_map/psum | solution.py:98
  598.0 1.7 copy.35
  599.7 1.7 copy.36
  (88 shorter events, 43.0 us)
Async XLA Ops:
  7.2 438.4 %copy-start = (bf16[256,256]{1,0:T(8,128)(2,1)S(1)}, bf16[256,256]{1,0:T(8,128)(2,1)}, u32[]{:S(2)}) copy-start(bf16[256,256]{1,0:T(8,128)(2,1)} %param.16) | copy-start | bytes 393220
  7.2 438.4 %reduce-scatter.2.cloned.1.call-start = ((), (), s32[]{:S(2)}) async-start(), calls=%async_computation.1 | async-start | bytes 1966080 | tf_op jit(solution)/shard_map/reduce_scatter | solution.py:84
  7.2 23.0 %collective-permute-start.1 = (bf16[1536,256]{1,0:T(8,128)(2,1)}, bf16[1536,256]{1,0:T(8,128)(2,1)S(1)}, u32[]{:S(2)}, u32[]{:S(2)}) collective-permute-start(bf16[1536,256]{1,0:T(8,128)(2,1)} %param.10), channel_id=1, source_target_pairs={{112,0},{116,4},{120,8},{124,12},{0,16},{4,20},{8,24},{12,28},{16,... | collective-permute-start | bytes 2359304 | tf_op jit(solution)/shard_map/ppermute | solution.py:10
  30.3 19.4 %collective-permute-start.2 = (bf16[1536,256]{1,0:T(8,128)(2,1)S(1)}, bf16[1536,256]{1,0:T(8,128)(2,1)S(1)}, u32[]{:S(2)}, u32[]{:S(2)}) collective-permute-start(bf16[1536,256]{1,0:T(8,128)(2,1)S(1)} %collective-permute-done.1), channel_id=1, source_target_pairs={{32,0},{36,4},{40,8},{44,12},{48,16},{52,20},{56,24},{60,28},{64,3... | collective-permute-start | bytes 2359304 | tf_op jit(solution)/shard_map/ppermute | solution.py:10
  49.7 17.1 %collective-permute-start.3 = (bf16[1536,256]{1,0:T(8,128)(2,1)S(1)}, bf16[1536,256]{1,0:T(8,128)(2,1)S(1)}, u32[]{:S(2)}, u32[]{:S(2)}) collective-permute-start(bf16[1536,256]{1,0:T(8,128)(2,1)S(1)} %broadcast_select_fusion), channel_id=1, source_target_pairs={{64,0},{68,4},{72,8},{76,12},{80,16},{84,20},{88,24},{92,28},{96,3... | collective-permute-start | bytes 2359304 | tf_op jit(solution)/shard_map/ppermute | solution.py:10
  69.0 44.4 %collective-permute-start = (bf16[1536,256]{1,0:T(8,128)(2,1)S(1)}, bf16[1536,256]{1,0:T(8,128)(2,1)}, u32[]{:S(2)}, u32[]{:S(2)}) collective-permute-start(bf16[1536,256]{1,0:T(8,128)(2,1)S(1)} %copy.28), channel_id=1, source_target_pairs={{4,0},{8,4},{12,8},{16,12},{20,16},{24,20},{28,24},{32,28},{36,32}... | collective-permute-start | bytes 2359304 | tf_op jit(solution)/shard_map/while/body/eval_jaxpr/ppermute | solution.py:10
  85.2 16.1 %copy-start.3 = (s32[8]{0:T(128)S(1)}, s32[8]{0:T(128)}, u32[]{:S(2)}) copy-start(s32[8]{0:T(128)} %get-tuple-element.243) | copy-start | bytes 100 | tf_op jit(solution)/shard_map/while
  114.5 41.4 %collective-permute-start = (bf16[1536,256]{1,0:T(8,128)(2,1)S(1)}, bf16[1536,256]{1,0:T(8,128)(2,1)}, u32[]{:S(2)}, u32[]{:S(2)}) collective-permute-start(bf16[1536,256]{1,0:T(8,128)(2,1)S(1)} %copy.28), channel_id=1, source_target_pairs={{4,0},{8,4},{12,8},{16,12},{20,16},{24,20},{28,24},{32,28},{36,32}... | collective-permute-start | bytes 2359304 | tf_op jit(solution)/shard_map/while/body/eval_jaxpr/ppermute | solution.py:10
  127.2 16.1 %copy-start.3 = (s32[8]{0:T(128)S(1)}, s32[8]{0:T(128)}, u32[]{:S(2)}) copy-start(s32[8]{0:T(128)} %get-tuple-element.243) | copy-start | bytes 100 | tf_op jit(solution)/shard_map/while
  157.0 41.1 %collective-permute-start = (bf16[1536,256]{1,0:T(8,128)(2,1)S(1)}, bf16[1536,256]{1,0:T(8,128)(2,1)}, u32[]{:S(2)}, u32[]{:S(2)}) collective-permute-start(bf16[1536,256]{1,0:T(8,128)(2,1)S(1)} %copy.28), channel_id=1, source_target_pairs={{4,0},{8,4},{12,8},{16,12},{20,16},{24,20},{28,24},{32,28},{36,32}... | collective-permute-start | bytes 2359304 | tf_op jit(solution)/shard_map/while/body/eval_jaxpr/ppermute | solution.py:10
  169.4 16.1 %copy-start.3 = (s32[8]{0:T(128)S(1)}, s32[8]{0:T(128)}, u32[]{:S(2)}) copy-start(s32[8]{0:T(128)} %get-tuple-element.243) | copy-start | bytes 100 | tf_op jit(solution)/shard_map/while
  199.2 41.1 %collective-permute-start = (bf16[1536,256]{1,0:T(8,128)(2,1)S(1)}, bf16[1536,256]{1,0:T(8,128)(2,1)}, u32[]{:S(2)}, u32[]{:S(2)}) collective-permute-start(bf16[1536,256]{1,0:T(8,128)(2,1)S(1)} %copy.28), channel_id=1, source_target_pairs={{4,0},{8,4},{12,8},{16,12},{20,16},{24,20},{28,24},{32,28},{36,32}... | collective-permute-start | bytes 2359304 | tf_op jit(solution)/shard_map/while/body/eval_jaxpr/ppermute | solution.py:10
  211.7 16.1 %copy-start.3 = (s32[8]{0:T(128)S(1)}, s32[8]{0:T(128)}, u32[]{:S(2)}) copy-start(s32[8]{0:T(128)} %get-tuple-element.243) | copy-start | bytes 100 | tf_op jit(solution)/shard_map/while
  241.5 43.5 %collective-permute-start = (bf16[1536,256]{1,0:T(8,128)(2,1)S(1)}, bf16[1536,256]{1,0:T(8,128)(2,1)}, u32[]{:S(2)}, u32[]{:S(2)}) collective-permute-start(bf16[1536,256]{1,0:T(8,128)(2,1)S(1)} %copy.28), channel_id=1, source_target_pairs={{4,0},{8,4},{12,8},{16,12},{20,16},{24,20},{28,24},{32,28},{36,32}... | collective-permute-start | bytes 2359304 | tf_op jit(solution)/shard_map/while/body/eval_jaxpr/ppermute | solution.py:10
  256.3 16.1 %copy-start.3 = (s32[8]{0:T(128)S(1)}, s32[8]{0:T(128)}, u32[]{:S(2)}) copy-start(s32[8]{0:T(128)} %get-tuple-element.243) | copy-start | bytes 100 | tf_op jit(solution)/shard_map/while
  286.1 41.4 %collective-permute-start = (bf16[1536,256]{1,0:T(8,128)(2,1)S(1)}, bf16[1536,256]{1,0:T(8,128)(2,1)}, u32[]{:S(2)}, u32[]{:S(2)}) collective-permute-start(bf16[1536,256]{1,0:T(8,128)(2,1)S(1)} %copy.28), channel_id=1, source_target_pairs={{4,0},{8,4},{12,8},{16,12},{20,16},{24,20},{28,24},{32,28},{36,32}... | collective-permute-start | bytes 2359304 | tf_op jit(solution)/shard_map/while/body/eval_jaxpr/ppermute | solution.py:10
  298.8 16.1 %copy-start.3 = (s32[8]{0:T(128)S(1)}, s32[8]{0:T(128)}, u32[]{:S(2)}) copy-start(s32[8]{0:T(128)} %get-tuple-element.243) | copy-start | bytes 100 | tf_op jit(solution)/shard_map/while
  328.6 41.1 %collective-permute-start = (bf16[1536,256]{1,0:T(8,128)(2,1)S(1)}, bf16[1536,256]{1,0:T(8,128)(2,1)}, u32[]{:S(2)}, u32[]{:S(2)}) collective-permute-start(bf16[1536,256]{1,0:T(8,128)(2,1)S(1)} %copy.28), channel_id=1, source_target_pairs={{4,0},{8,4},{12,8},{16,12},{20,16},{24,20},{28,24},{32,28},{36,32}... | collective-permute-start | bytes 2359304 | tf_op jit(solution)/shard_map/while/body/eval_jaxpr/ppermute | solution.py:10
  341.1 16.1 %copy-start.3 = (s32[8]{0:T(128)S(1)}, s32[8]{0:T(128)}, u32[]{:S(2)}) copy-start(s32[8]{0:T(128)} %get-tuple-element.243) | copy-start | bytes 100 | tf_op jit(solution)/shard_map/while
  395.3 10.0 %copy-start.1 = (f32[1536,256]{1,0:T(8,128)S(1)}, f32[1536,256]{1,0:T(8,128)}, u32[]{:S(2)}) copy-start(f32[1536,256]{1,0:T(8,128)} %get-tuple-element.128) | copy-start | bytes 4718596
  403.5 3.3 copy-start.2
  406.7 191.2 %all-reduce.3.cloned.1.call-start = ((), (), s32[]{:S(2)}) async-start(), calls=%async_computation.2 | async-start | bytes 1048576 | tf_op jit(solution)/shard_map/psum | solution.py:98
Sparse Core Ops, SparseCore 0:
  406.9 38.6 reduce-scatter.1
  451.7 146.2 all-reduce.2
where the time goes:
time: 610 us; the launch traced here: 608 us
  waiting for transfers between devices  237 us (39%)
  local copies, waits for them, and re-layouts  177 us (29%)
  matrix products  139 us (23%)
  other arithmetic  29.8 us (5%)
  between operations  14.1 us (2%)
  starting transfers between devices  11.7 us (2%)
    psum x1, waiting for transfers between devices, on_device(): grad_self, grad_neigh = lax.psum((self_term, neigh_term), ('dom', 'rep'))  146 us
    while x35, local copies, waits for them, and re-layouts  132 us
    dot_general x8, matrix products, step_terms(): jnp.einsum('kij,kjf->kif', weights_now, picked, preferred_element_type=jn...  63.2 us
    dot_general x8, matrix products, step_terms(): jnp.dot(placing, product.reshape(slot_total, tile_side * width), precisio...  55 us
    ppermute x10, waiting for transfers between devices, passed_along(): return lax.ppermute(block, axis, route)  52.5 us
    reduce_scatter x1, waiting for transfers between devices, on_device(): lax.psum_scatter(partial_value, 'rep', scatter_dimension=0, tiled=True)  37.6 us
    add x7, other arithmetic, turn_one(): partial_value = partial_value + contribution(current, turn_index)  22.1 us
    unnamed x10, local copies, waits for them, and re-layouts  17.1 us
  transfers between devices with their start and end apart: 12, of which 5 were waited for; matrix products, arithmetic and copies ran while one was open for 48% of the time, Pallas kernels for 0%

commit v1 on v0

--- a/solution.py
+++ b/solution.py
@@ -2,6 +2,11 @@
 import jax.numpy as jnp
 from jax import lax
 from jax.sharding import PartitionSpec as P
+
+
+def axis_by_axis(value, inner_axis, outer_axis):
+    half = lax.psum(value, inner_axis)
+    return lax.psum(half, outer_axis)
 
 
 def passed_along(block, axis, distance):
@@ -95,7 +100,7 @@
     )
     self_term = jnp.einsum("nf,ng->fg", own_rows, slope, preferred_element_type=jnp.float32)
     neigh_term = jnp.einsum("nf,ng->fg", aggregate, slope, preferred_element_type=jnp.float32)
-    grad_self, grad_neigh = lax.psum((self_term, neigh_term), ("dom", "rep"))
+    grad_self, grad_neigh = axis_by_axis((self_term, neigh_term), "dom", "rep")
     return (output, grad_self, grad_neigh)
 
 

time: 610 us -> 819 us (1.34)
  waiting for transfers between devices: 237 us -> 446 us
    psum x1 -> x2, waiting for transfers between devices: 146 us -> 355 us  [the longest x1 289 us: axis_by_axis(): half = lax.psum(value, inner_axis)]
  transfers between devices with their start and end apart: 12 -> 13, of which waited for: 5 -> 6; matrix products, arithmetic and copies ran while one was open for 48% -> 36% of each run, Pallas kernels for 0% -> 0%
where the time goes in v1:
time: 819 us; the launch traced here: 817 us
  waiting for transfers between devices  446 us (54%)
  local copies, waits for them, and re-layouts  177 us (22%)
  matrix products  139 us (17%)
  other arithmetic  29.9 us (4%)
  between operations  13.8 us (2%)
  starting transfers between devices  11.7 us (1%)
    psum x1, waiting for transfers between devices, axis_by_axis(): half = lax.psum(value, inner_axis)  289 us
    while x35, local copies, waits for them, and re-layouts  132 us
    psum x1, waiting for transfers between devices, axis_by_axis(): return lax.psum(half, outer_axis)  66.8 us
    dot_general x8, matrix products, step_terms(): jnp.einsum('kij,kjf->kif', weights_now, picked, preferred_element_type=jn...  63.2 us
    dot_general x8, matrix products, step_terms(): jnp.dot(placing, product.reshape(slot_total, tile_side * width), precisio...  55 us
    ppermute x10, waiting for transfers between devices, passed_along(): return lax.ppermute(block, axis, route)  52.5 us
    reduce_scatter x1, waiting for transfers between devices, on_device(): lax.psum_scatter(partial_value, 'rep', scatter_dimension=0, tiled=True)  37.6 us
    add x7, other arithmetic, turn_one(): partial_value = partial_value + contribution(current, turn_index)  22.2 us
  transfers between devices with their start and end apart: 13, of which 6 were waited for; matrix products, arithmetic and copies ran while one was open for 36% of the time, Pallas kernels for 0%

profile of v1, /device:TPU:1, one launch (start us, length us, event | category | flops | bytes accessed | tf_op | source)
XLA Modules:
  0.0 817.0 jit_solution(10863706267927850097)
XLA Ops:
  7.2 2.5 collective-permute-start.1
  9.7 20.5 %collective-permute-done.1 = bf16[1536,256]{1,0:T(8,128)(2,1)S(1)} collective-permute-done((bf16[1536,256]{1,0:T(8,128)(2,1)}, bf16[1536,256]{1,0:T(8,128)(2,1)S(1)}, u32[]{:S(2)}, u32[]{:S(2)}) %collective-permute-start.1) | collective-permute-done | bytes 786464 | tf_op jit(solution)/shard_map/ppermute | solution.py:15
  31.3 18.3 %collective-permute-done.2 = bf16[1536,256]{1,0:T(8,128)(2,1)S(1)} collective-permute-done((bf16[1536,256]{1,0:T(8,128)(2,1)S(1)}, bf16[1536,256]{1,0:T(8,128)(2,1)S(1)}, u32[]{:S(2)}, u32[]{:S(2)}) %collective-permute-start.2) | collective-permute-done | bytes 786464 | tf_op jit(solution)/shard_map/ppermute | solution.py:15
  53.1 13.7 %collective-permute-done.3 = bf16[1536,256]{1,0:T(8,128)(2,1)S(1)} collective-permute-done((bf16[1536,256]{1,0:T(8,128)(2,1)S(1)}, bf16[1536,256]{1,0:T(8,128)(2,1)S(1)}, u32[]{:S(2)}, u32[]{:S(2)}) %collective-permute-start.3) | collective-permute-done | bytes 786464 | tf_op jit(solution)/shard_map/ppermute | solution.py:15
  67.8 302.1 %while.16 = (s32[]{:T(128)}, bf16[1536,256]{1,0:T(8,128)(2,1)}, f32[1536,256]{1,0:T(8,128)}, s32[8,88]{1,0:T(8,128)}, s32[8]{0:T(128)}, /*index=5*/bf16[8,88,128...) while((s32[]{:T(128)}, bf16[1536,256]{1,0:T(8,128)(2,1)}, f32[1536,256]{1,0:T(8,128)}, ...), condition=%wide.region_1.2_spmd.clone, body=%wide.region_0.1_spmd.clone.sunk | while | flops 1226312832 | bytes 88607792 | solution.py:87
  68.9 3.9 collective-permute-start
  74.1 1.7 convolution_convert_fusion.3
  75.8 1.5 copy.22
  77.4 7.8 fusion.53
  85.2 16.1 %copy.23 = f32[11,8,128,256]{3,1,2,0:T(8,128)} copy(f32[11,8,128,256]{3,2,1,0:T(8,128)} %bitcast.62) | data formatting | bytes 23068672 | tf_op jit(solution)/shard_map/while
  102.5 6.7 fusion.54
  110.6 2.8 select_add_fusion.2
  116.2 1.7 convolution_convert_fusion.3
  117.9 1.5 copy.22
  119.4 7.8 fusion.53
  127.2 16.1 %copy.23 = f32[11,8,128,256]{3,1,2,0:T(8,128)} copy(f32[11,8,128,256]{3,2,1,0:T(8,128)} %bitcast.62) | data formatting | bytes 23068672 | tf_op jit(solution)/shard_map/while
  144.6 6.7 fusion.54
  152.7 3.2 select_add_fusion.2
  158.5 1.7 convolution_convert_fusion.3
  160.1 1.5 copy.22
  161.7 7.8 fusion.53
  169.5 16.1 %copy.23 = f32[11,8,128,256]{3,1,2,0:T(8,128)} copy(f32[11,8,128,256]{3,2,1,0:T(8,128)} %bitcast.62) | data formatting | bytes 23068672 | tf_op jit(solution)/shard_map/while
  186.9 6.7 fusion.54
  194.9 3.2 select_add_fusion.2
  200.7 1.7 convolution_convert_fusion.3
  202.4 1.5 copy.22
  203.9 7.8 fusion.53
  211.7 16.1 %copy.23 = f32[11,8,128,256]{3,1,2,0:T(8,128)} copy(f32[11,8,128,256]{3,2,1,0:T(8,128)} %bitcast.62) | data formatting | bytes 23068672 | tf_op jit(solution)/shard_map/while
  229.1 6.7 fusion.54
  237.2 3.2 select_add_fusion.2
  241.5 2.6 collective-permute-start
  245.4 1.7 convolution_convert_fusion.3
  247.1 1.5 copy.22
  248.6 7.8 fusion.53
  256.4 16.1 %copy.23 = f32[11,8,128,256]{3,1,2,0:T(8,128)} copy(f32[11,8,128,256]{3,2,1,0:T(8,128)} %bitcast.62) | data formatting | bytes 23068672 | tf_op jit(solution)/shard_map/while
  273.8 6.7 fusion.54
  281.8 3.2 select_add_fusion.2
  287.9 1.7 convolution_convert_fusion.3
  289.6 1.5 copy.22
  291.1 7.8 fusion.53
  299.0 16.1 %copy.23 = f32[11,8,128,256]{3,1,2,0:T(8,128)} copy(f32[11,8,128,256]{3,2,1,0:T(8,128)} %bitcast.62) | data formatting | bytes 23068672 | tf_op jit(solution)/shard_map/while
  316.3 6.7 fusion.54
  324.4 3.2 select_add_fusion.2
  330.2 1.7 convolution_convert_fusion.3
  331.9 1.5 copy.22
  333.4 7.8 fusion.53
  341.2 16.1 %copy.23 = f32[11,8,128,256]{3,1,2,0:T(8,128)} copy(f32[11,8,128,256]{3,2,1,0:T(8,128)} %bitcast.62) | data formatting | bytes 23068672 | tf_op jit(solution)/shard_map/while
  358.6 6.7 fusion.54
  366.6 3.2 select_add_fusion.2
  369.9 1.6 reshape.66
  371.4 1.7 convolution_convert_fusion.1
  373.1 1.5 copy.17
  374.7 8.6 %convolution_bitcast_fusion = f32[88,128,256]{1,2,0:T(8,128)} fusion(bf16[88,128,256]{2,1,0:T(8,128)(2,1)S(1)} %bitcast.68, bf16[1,1,8,88,128,128]{5,4,3,2,1,0:T(8,128)(2,1)} %bitcast.70), kind=kOutput, calls=%fused_computation.19 | convolution fusion | flops 738197504 | bytes 20185088 | tf_op jit(solution)/shard_map/kij,kjf->kif/dot_general | solution.py:32
  383.3 12.2 %copy.18 = f32[11,8,128,256]{3,1,2,0:T(8,128)} copy(f32[11,8,128,256]{2,3,1,0:T(8,128)} %bitcast.66) | data formatting | bytes 23068672
  395.5 8.1 fusion.23
  403.6 1.9 reshape.69
  408.1 37.6 %reduce-scatter.2.cloned.1.call-done = f32[384,256]{1,0:T(8,128)} async-done(((f32[1536,256]{1,0:T(8,128)}), f32[384,256]{1,0:T(8,128)}) %reduce-scatter.2.cloned.1.call-update) | async-done | bytes 393232 | tf_op jit(solution)/shard_map/reduce_scatter | solution.py:89
  445.7 2.1 multiply_convert_fusion
  447.7 1.9 fusion.14
  449.6 2.0 fusion.18
  451.7 288.6 %all-reduce.5.cloned.1.call-done = (f32[256,256]{1,0:T(8,128)}, f32[256,256]{1,0:T(8,128)}) async-done(((f32[256,256]{1,0:T(8,128)}, f32[256,256]{1,0:T(8,128)}), (f32[256,256]{1,0:T(8,128)}, f32[256,256]{1,0:T(8,128)})) %all-reduce.5.cloned.1.call-update) | async-done | bytes 524304 | tf_op jit(solution)/shard_map/psum | solution.py:8
  740.3 66.8 %all-reduce.7.cloned.1.call-done = (f32[256,256]{1,0:T(8,128)}, f32[256,256]{1,0:T(8,128)}) async-done(((f32[256,256]{1,0:T(8,128)}, f32[256,256]{1,0:T(8,128)}), (f32[256,256]{1,0:T(8,128)}, f32[256,256]{1,0:T(8,128)})) %all-reduce.7.cloned.1.call-update) | async-done | bytes 524304 | tf_op jit(solution)/shard_map/psum | solution.py:9
  807.1 1.7 copy.37
  808.8 1.7 copy.38
  (91 shorter events, 44.4 us)
Async XLA Ops:
  7.2 438.5 %copy-start = (bf16[256,256]{1,0:T(8,128)(2,1)S(1)}, bf16[256,256]{1,0:T(8,128)(2,1)}, u32[]{:S(2)}) copy-start(bf16[256,256]{1,0:T(8,128)(2,1)} %param.16) | copy-start | bytes 393220
  7.2 438.5 %reduce-scatter.2.cloned.1.call-start = ((), (), s32[]{:S(2)}) async-start(), calls=%async_computation.1 | async-start | bytes 1966080 | tf_op jit(solution)/shard_map/reduce_scatter | solution.py:89
  7.2 23.0 %collective-permute-start.1 = (bf16[1536,256]{1,0:T(8,128)(2,1)}, bf16[1536,256]{1,0:T(8,128)(2,1)S(1)}, u32[]{:S(2)}, u32[]{:S(2)}) collective-permute-start(bf16[1536,256]{1,0:T(8,128)(2,1)} %param.10), channel_id=1, source_target_pairs={{112,0},{116,4},{120,8},{124,12},{0,16},{4,20},{8,24},{12,28},{16,... | collective-permute-start | bytes 2359304 | tf_op jit(solution)/shard_map/ppermute | solution.py:15
  30.3 19.4 %collective-permute-start.2 = (bf16[1536,256]{1,0:T(8,128)(2,1)S(1)}, bf16[1536,256]{1,0:T(8,128)(2,1)S(1)}, u32[]{:S(2)}, u32[]{:S(2)}) collective-permute-start(bf16[1536,256]{1,0:T(8,128)(2,1)S(1)} %collective-permute-done.1), channel_id=1, source_target_pairs={{32,0},{36,4},{40,8},{44,12},{48,16},{52,20},{56,24},{60,28},{64,3... | collective-permute-start | bytes 2359304 | tf_op jit(solution)/shard_map/ppermute | solution.py:15
  49.7 17.1 %collective-permute-start.3 = (bf16[1536,256]{1,0:T(8,128)(2,1)S(1)}, bf16[1536,256]{1,0:T(8,128)(2,1)S(1)}, u32[]{:S(2)}, u32[]{:S(2)}) collective-permute-start(bf16[1536,256]{1,0:T(8,128)(2,1)S(1)} %broadcast_select_fusion), channel_id=1, source_target_pairs={{64,0},{68,4},{72,8},{76,12},{80,16},{84,20},{88,24},{92,28},{96,3... | collective-permute-start | bytes 2359304 | tf_op jit(solution)/shard_map/ppermute | solution.py:15
  68.9 44.4 %collective-permute-start = (bf16[1536,256]{1,0:T(8,128)(2,1)S(1)}, bf16[1536,256]{1,0:T(8,128)(2,1)}, u32[]{:S(2)}, u32[]{:S(2)}) collective-permute-start(bf16[1536,256]{1,0:T(8,128)(2,1)S(1)} %copy.28), channel_id=1, source_target_pairs={{4,0},{8,4},{12,8},{16,12},{20,16},{24,20},{28,24},{32,28},{36,32}... | collective-permute-start | bytes 2359304 | tf_op jit(solution)/shard_map/while/body/eval_jaxpr/ppermute | solution.py:15
  85.2 16.1 %copy-start.3 = (s32[8]{0:T(128)S(1)}, s32[8]{0:T(128)}, u32[]{:S(2)}) copy-start(s32[8]{0:T(128)} %get-tuple-element.245) | copy-start | bytes 100 | tf_op jit(solution)/shard_map/while
  114.5 41.4 %collective-permute-start = (bf16[1536,256]{1,0:T(8,128)(2,1)S(1)}, bf16[1536,256]{1,0:T(8,128)(2,1)}, u32[]{:S(2)}, u32[]{:S(2)}) collective-permute-start(bf16[1536,256]{1,0:T(8,128)(2,1)S(1)} %copy.28), channel_id=1, source_target_pairs={{4,0},{8,4},{12,8},{16,12},{20,16},{24,20},{28,24},{32,28},{36,32}... | collective-permute-start | bytes 2359304 | tf_op jit(solution)/shard_map/while/body/eval_jaxpr/ppermute | solution.py:15
  127.2 16.1 %copy-start.3 = (s32[8]{0:T(128)S(1)}, s32[8]{0:T(128)}, u32[]{:S(2)}) copy-start(s32[8]{0:T(128)} %get-tuple-element.245) | copy-start | bytes 100 | tf_op jit(solution)/shard_map/while
  157.0 41.1 %collective-permute-start = (bf16[1536,256]{1,0:T(8,128)(2,1)S(1)}, bf16[1536,256]{1,0:T(8,128)(2,1)}, u32[]{:S(2)}, u32[]{:S(2)}) collective-permute-start(bf16[1536,256]{1,0:T(8,128)(2,1)S(1)} %copy.28), channel_id=1, source_target_pairs={{4,0},{8,4},{12,8},{16,12},{20,16},{24,20},{28,24},{32,28},{36,32}... | collective-permute-start | bytes 2359304 | tf_op jit(solution)/shard_map/while/body/eval_jaxpr/ppermute | solution.py:15
  169.5 16.1 %copy-start.3 = (s32[8]{0:T(128)S(1)}, s32[8]{0:T(128)}, u32[]{:S(2)}) copy-start(s32[8]{0:T(128)} %get-tuple-element.245) | copy-start | bytes 100 | tf_op jit(solution)/shard_map/while
  199.3 41.1 %collective-permute-start = (bf16[1536,256]{1,0:T(8,128)(2,1)S(1)}, bf16[1536,256]{1,0:T(8,128)(2,1)}, u32[]{:S(2)}, u32[]{:S(2)}) collective-permute-start(bf16[1536,256]{1,0:T(8,128)(2,1)S(1)} %copy.28), channel_id=1, source_target_pairs={{4,0},{8,4},{12,8},{16,12},{20,16},{24,20},{28,24},{32,28},{36,32}... | collective-permute-start | bytes 2359304 | tf_op jit(solution)/shard_map/while/body/eval_jaxpr/ppermute | solution.py:15
  211.7 16.1 %copy-start.3 = (s32[8]{0:T(128)S(1)}, s32[8]{0:T(128)}, u32[]{:S(2)}) copy-start(s32[8]{0:T(128)} %get-tuple-element.245) | copy-start | bytes 100 | tf_op jit(solution)/shard_map/while
  241.5 43.5 %collective-permute-start = (bf16[1536,256]{1,0:T(8,128)(2,1)S(1)}, bf16[1536,256]{1,0:T(8,128)(2,1)}, u32[]{:S(2)}, u32[]{:S(2)}) collective-permute-start(bf16[1536,256]{1,0:T(8,128)(2,1)S(1)} %copy.28), channel_id=1, source_target_pairs={{4,0},{8,4},{12,8},{16,12},{20,16},{24,20},{28,24},{32,28},{36,32}... | collective-permute-start | bytes 2359304 | tf_op jit(solution)/shard_map/while/body/eval_jaxpr/ppermute | solution.py:15
  256.4 16.1 %copy-start.3 = (s32[8]{0:T(128)S(1)}, s32[8]{0:T(128)}, u32[]{:S(2)}) copy-start(s32[8]{0:T(128)} %get-tuple-element.245) | copy-start | bytes 100 | tf_op jit(solution)/shard_map/while
  286.2 41.4 %collective-permute-start = (bf16[1536,256]{1,0:T(8,128)(2,1)S(1)}, bf16[1536,256]{1,0:T(8,128)(2,1)}, u32[]{:S(2)}, u32[]{:S(2)}) collective-permute-start(bf16[1536,256]{1,0:T(8,128)(2,1)S(1)} %copy.28), channel_id=1, source_target_pairs={{4,0},{8,4},{12,8},{16,12},{20,16},{24,20},{28,24},{32,28},{36,32}... | collective-permute-start | bytes 2359304 | tf_op jit(solution)/shard_map/while/body/eval_jaxpr/ppermute | solution.py:15
  298.9 16.1 %copy-start.3 = (s32[8]{0:T(128)S(1)}, s32[8]{0:T(128)}, u32[]{:S(2)}) copy-start(s32[8]{0:T(128)} %get-tuple-element.245) | copy-start | bytes 100 | tf_op jit(solution)/shard_map/while
  328.8 41.1 %collective-permute-start = (bf16[1536,256]{1,0:T(8,128)(2,1)S(1)}, bf16[1536,256]{1,0:T(8,128)(2,1)}, u32[]{:S(2)}, u32[]{:S(2)}) collective-permute-start(bf16[1536,256]{1,0:T(8,128)(2,1)S(1)} %copy.28), channel_id=1, source_target_pairs={{4,0},{8,4},{12,8},{16,12},{20,16},{24,20},{28,24},{32,28},{36,32}... | collective-permute-start | bytes 2359304 | tf_op jit(solution)/shard_map/while/body/eval_jaxpr/ppermute | solution.py:15
  341.2 16.1 %copy-start.3 = (s32[8]{0:T(128)S(1)}, s32[8]{0:T(128)}, u32[]{:S(2)}) copy-start(s32[8]{0:T(128)} %get-tuple-element.245) | copy-start | bytes 100 | tf_op jit(solution)/shard_map/while
  395.5 10.0 %copy-start.1 = (f32[1536,256]{1,0:T(8,128)S(1)}, f32[1536,256]{1,0:T(8,128)}, u32[]{:S(2)}) copy-start(f32[1536,256]{1,0:T(8,128)} %get-tuple-element.128) | copy-start | bytes 4718596
  403.6 3.3 copy-start.2
  406.9 333.4 %all-reduce.5.cloned.1.call-start = ((), (), s32[]{:S(2)}) async-start(), calls=%async_computation.2 | async-start | bytes 1048576 | tf_op jit(solution)/shard_map/psum | solution.py:8
  451.6 355.5 %all-reduce.7.cloned.1.call-start = ((), (), s32[]{:S(2)}) async-start(), calls=%async_computation.3 | async-start | bytes 1048576 | tf_op jit(solution)/shard_map/psum | solution.py:9
Sparse Core Ops, SparseCore 0:
  407.0 38.5 reduce-scatter.1
  451.8 288.5 all-reduce.4
  742.9 64.1 all-reduce.6
